TPU v7x, 512 devices: a whole 4x8x8 slice. The times are simulated.
512 devices in a mesh: shot: 8 (over z_hi, x), recv: 8 (over y), surf: 8 (over z_lo, core).
Axes of the slice: x: 4, y: 8, z: 8 (z_hi: 2, z_lo: 4; z = z_hi * 4 + z_lo), core: 2. Of those that a mesh axis runs over, the one named last changes fastest.
Arguments:
- shot_data: bfloat16 [8, 2, 6144, 2048], P(None, None, ('surf', 'recv'), 'shot'), may hold values from -6 to 6
- recv_data: bfloat16 [8, 2, 6144, 2048], P(None, None, ('surf', 'shot'), 'recv'), may hold values from -0.078125 to 0.078125
- shot_offset: int32 [2048], P('shot'), may hold values from -256 to 255
- recv_offset: int32 [2048], P('recv'), may hold values from -256 to 255
- shot_taper_index: int32 [2048], P('shot'), may hold values from 0 to 3
- receiver_taper_index: int32 [2048], P('recv'), may hold values from 0 to 3
Outputs:
- predicted: float32 [8, 2, 2048, 2048], P('surf', None, 'shot', 'recv')
All inputs are finite; a program needn't handle non-finite values.
Results may differ from a plain program's by a relative error of at most 0.0003.
Values may be sent and summed in bfloat16 or wider, within the bound.
A program may use at most 64 MiB of HBM per device.

v0:
```python
import jax
import jax.numpy as jnp
from jax import lax
from jax.sharding import PartitionSpec as P

R = 2048


def panel_product(left_operand, right_operand):
    real_real = jnp.einsum(
        "xaq,xad->xqd", left_operand[:, 0], right_operand[:, 0], preferred_element_type=jnp.float32
    )
    imag_imag = jnp.einsum(
        "xaq,xad->xqd", left_operand[:, 1], right_operand[:, 1], preferred_element_type=jnp.float32
    )
    real_imag = jnp.einsum(
        "xaq,xad->xqd", left_operand[:, 0], right_operand[:, 1], preferred_element_type=jnp.float32
    )
    imag_real = jnp.einsum(
        "xaq,xad->xqd", left_operand[:, 1], right_operand[:, 0], preferred_element_type=jnp.float32
    )
    return jnp.stack([real_real - imag_imag, real_imag + imag_real], axis=1)


def make_folder(right_full, piece):
    return panel_product(piece, right_full)


def on_device(
    shot_data, recv_data, shot_offset, recv_offset, shot_taper_index, receiver_taper_index
):
    right_full = lax.all_gather(recv_data, "shot", axis=2, tiled=True)
    partial_sum = make_folder(right_full, lax.all_gather(shot_data, "recv", axis=2, tiled=True))
    multiples = lax.psum_scatter(partial_sum, "surf", scatter_dimension=0, tiled=True)
    shot_row_block = shot_offset.shape[0]
    recv_cols = recv_offset.shape[0]
    shot_pos = (
        lax.axis_index("shot") * shot_row_block
        + jnp.arange(shot_row_block, dtype=jnp.int32)
        + shot_offset
    )
    recv_pos = (
        lax.axis_index("recv") * recv_cols + jnp.arange(recv_cols, dtype=jnp.int32) + recv_offset
    )
    distance = jnp.abs(recv_pos[None, :] - shot_pos[:, None])
    half_width = R // 8 * (2 + shot_taper_index[:, None] + receiver_taper_index[None, :])
    ratio = jnp.minimum(distance, half_width).astype(jnp.float32) / half_width.astype(jnp.float32)
    taper = 0.5 * (1.0 + jnp.cos(jnp.pi * ratio))
    return multiples * taper[None, None, :, :]


def solution(mesh):
    placed = (
        P(None, None, ("surf", "recv"), "shot"),
        P(None, None, ("surf", "shot"), "recv"),
        P("shot"),
        P("recv"),
        P("shot"),
        P("recv"),
    )
    return jax.shard_map(
        on_device,
        mesh=mesh,
        in_specs=placed,
        out_specs=P("surf", None, "shot", "recv"),
        check_vma=False,
    )
```

profile of v0, /device:TPU:2, one launch (start us, length us, event | category | flops | bytes accessed | tf_op | source)
XLA Modules:
  0.0 370.5 jit_solution(3620094551108705786)
XLA Ops:
  6.5 0.0 all-gather.3.cloned.1.call-start
  6.5 2.5 copy.10
  9.1 0.0 all-gather.3.cloned.1.call-update
  9.1 0.0 all-gather.5.cloned.1.call-start
  9.1 2.1 copy.12
  11.2 0.0 all-gather.5.cloned.1.call-update
  11.2 0.0 all-reduce.3.cloned.1.call-start
  11.3 79.5 %all-gather.3.cloned.1.call-done = bf16[8,2,768,256]{3,0,1,2:T(8,128)(2,1)} async-done(((bf16[8,2,96,256]{3,0,1,2:T(8,128)(2,1)}), bf16[8,2,768,256]{3,0,1,2:T(8,128)(2,1)}) %all-gather.3.cloned.1.call-update) | async-done | bytes 6291472 | tf_op jit(solution)/shard_map/all_gather | solution.py:33
  90.8 5.9 %fusion.13 = (bf16[8,1,768,256]{3,0,1,2:T(8,128)(2,1)}, bf16[8,1,768,256]{3,0,1,2:T(8,128)(2,1)}) fusion(bf16[8,2,768,256]{3,0,1,2:T(8,128)(2,1)} %all-gather.3.cloned.1.call-done), kind=kLoop, calls=%fused_computation.19 | loop fusion | bytes 12582912 | tf_op jit(solution)/shard_map/slice | solution.py:11
  96.7 3.8 %copy.17 = bf16[8,1,768,256]{2,3,0,1:T(8,128)(2,1)S(1)} copy(bf16[8,1,768,256]{3,0,1,2:T(8,128)(2,1)} %get-tuple-element.5) | data formatting | bytes 6291456
  100.5 5.0 %copy.18 = bf16[8,1,768,256]{2,3,0,1:T(8,128)(2,1)} copy(bf16[8,1,768,256]{3,0,1,2:T(8,128)(2,1)} %get-tuple-element.6) | data formatting | bytes 6291456
  105.5 131.8 %all-gather.5.cloned.1.call-done = bf16[8,2,768,256]{3,2,0,1:T(8,128)(2,1)} async-done(((bf16[8,2,96,256]{3,2,0,1:T(8,128)(2,1)}), bf16[8,2,768,256]{3,2,0,1:T(8,128)(2,1)}) %all-gather.5.cloned.1.call-update) | async-done | bytes 6291472 | tf_op jit(solution)/shard_map/all_gather | solution.py:32
  237.3 4.0 %fusion = f32[8,256,256]{2,1,0:T(8,128)S(1)} fusion(bf16[8,1,768,256]{2,3,0,1:T(8,128)(2,1)} %copy.18, bf16[8,2,768,256]{3,2,0,1:T(8,128)(2,1)} %all-gather.5.cloned.1.call-done), kind=kOutput, calls=%fused_computation.3 | convolution fusion | flops 805306368 | bytes 8388608 | tf_op jit(solution)/shard_map/xaq,xad->xqd/dot_general | solution.py:19
  241.3 0.7 copy-done
  242.0 2.9 fusion.2
  244.8 1.0 subtract_bitcast_fusion
  245.8 1.0 add_bitcast_fusion
  246.8 2.3 pad_maximum_fusion
  249.2 0.0 all-reduce.3.cloned.1.call-update
  249.2 1.3 dynamic-slice
  250.6 0.0 copy-done.1
  250.6 1.1 add_multiply_fusion
  251.7 109.8 %all-reduce.3.cloned.1.call-done = f32[8,2,256,256]{3,2,0,1:T(8,128)} async-done(((f32[8,2,256,256]{3,2,0,1:T(8,128)}), f32[8,2,256,256]{3,2,0,1:T(8,128)}) %all-reduce.3.cloned.1.call-update) | async-done | bytes 4194320
  361.5 2.5 fusion.12
  (10 shorter events, 0.0 us)
Async XLA Ops:
  6.5 84.3 %all-gather.3.cloned.1.call-start = ((), (), s32[]{:S(2)}) async-start(), calls=%async_computation | async-start | bytes 7077888 | tf_op jit(solution)/shard_map/all_gather | solution.py:33
  9.1 228.3 %all-gather.5.cloned.1.call-start = ((), (), s32[]{:S(2)}) async-start(), calls=%async_computation.1 | async-start | bytes 7077888 | tf_op jit(solution)/shard_map/all_gather | solution.py:32
  11.2 350.3 %all-reduce.3.cloned.1.call-start = ((), (), s32[]{:S(2)}) async-start(), calls=%async_computation.2 | async-start | bytes 8388608
  237.3 4.6 %copy-start = (bf16[8,2,768,256]{3,2,0,1:T(8,128)(2,1)S(1)}, bf16[8,2,768,256]{3,2,0,1:T(8,128)(2,1)}, u32[]{:S(2)}) copy-start(bf16[8,2,768,256]{3,2,0,1:T(8,128)(2,1)} %all-gather.5.cloned.1.call-done) | copy-start | bytes 18874372
  249.2 1.4 copy-start.4
  249.2 1.4 copy-start.2
  249.2 1.4 copy-start.3
  249.2 1.4 copy-start.1
Sparse Core Ops, SparseCore 0:
  9.4 81.3 all-gather.2
  93.9 143.3 all-gather.4
  249.3 112.1 all-reduce.2
where the time goes:
time: 371 us
  waiting for transfers between devices  321 us (87%)
  local copies, waits for them, and re-layouts  21.3 us (6%)
  between operations  13.2 us (4%)
  matrix products  8.78 us (2%)
  other arithmetic  5.95 us (2%)
    all_gather x1, waiting for transfers between devices, on_device(): right_full = lax.all_gather(recv_data, 'shot', axis=2, tiled=True)  132 us
    unnamed x4, waiting for transfers between devices  110 us
    all_gather x1, waiting for transfers between devices, on_device(): lax.all_gather(shot_data, 'recv', axis=2, tiled=True)  79.5 us
    unnamed x15, local copies, waits for them, and re-layouts  15.4 us
  transfers between devices with their start and end apart: 3, of which 3 were waited for; matrix products, arithmetic and copies ran while one was open for 5% of the time, Pallas kernels for 0%

commit v1 on v0

v1 whole, which is shorter than its diff:
```python
import jax
import jax.numpy as jnp
from jax import lax
from jax.experimental import pallas as pl
from jax.experimental.pallas import tpu as pltpu
from jax.sharding import PartitionSpec as P

R = 2048
MESH = pl.DeviceIdType.MESH
NEAR = ((0, 0), (0, 1), (1, 0), (1, 1), (3, 0), (3, 1), (2, 0), (2, 1))
FAR = ((2, 0), (2, 1), (3, 0), (3, 1), (1, 0), (1, 1), (0, 0), (0, 1))


def kernel(s_ref, r_ref, out_ref, a_buf, b_buf, acc, a_sem, b_sem, sa_sem, sb_sem, yr_sem, yl_sem, xr_sem, xl_sem):
    shot = lax.axis_index("shot")
    y = lax.axis_index("recv")
    u = lax.axis_index("surf")
    zh, x = shot // 4, shot % 4
    zl, c = u // 2, u % 2
    rows = s_ref.shape[2]
    half = 4 * rows

    def surf_of(step):
        b, e = step
        return ((zl + b) % 4) * 2 + (c + e) % 2

    def dest_of(step):
        b, e = step
        return ((zl + 4 - b) % 4) * 2 + (c + e) % 2

    def a_at(v, origin):
        return a_buf.at[v, :, pl.ds(pl.multiple_of(origin * rows, rows), rows), :]

    def b_at(v, origin):
        return b_buf.at[v, :, pl.ds(pl.multiple_of(origin * rows, rows), rows), :]

    def s_of(h, xx):
        return h * 4 + xx

    right = {"recv": (y + 1) % 8}
    left = {"recv": (y + 7) % 8}
    xright = {"shot": s_of(zh, (x + 1) % 4)}
    xleft = {"shot": s_of(zh, (x + 3) % 4)}
    other = s_of(1 - zh, x)

    barrier = pltpu.get_barrier_semaphore()
    peers = [right, left, xright, xleft]
    for step in NEAR:
        f = dest_of(step)
        if step != (0, 0):
            peers.append({"surf": f})
        peers.append({"shot": other, "surf": f})
    for peer in peers:
        pl.semaphore_signal(barrier, inc=1, device_id=peer, device_id_type=MESH)
    pl.semaphore_wait(barrier, len(peers))

    started = []

    def send(src, dst, send_sem, recv_sem, device):
        copy = pltpu.make_async_remote_copy(
            src_ref=src, dst_ref=dst, send_sem=send_sem, recv_sem=recv_sem, device_id=device, device_id_type=MESH
        )
        copy.start()
        started.append(copy)

    for i in range(8):
        if i == 0:
            pltpu.make_async_copy(s_ref.at[u], a_at(u, y), a_sem.at[u, y]).start()
            pltpu.make_async_copy(r_ref.at[u], b_at(u, shot), b_sem.at[u, shot]).start()
        else:
            f = dest_of(NEAR[i])
            send(s_ref.at[f], a_at(u, y), sa_sem.at[i], a_sem.at[u, y], {"surf": f})
            send(r_ref.at[f], b_at(u, shot), sb_sem.at[i], b_sem.at[u, shot], {"surf": f})
        f = dest_of(FAR[i])
        send(r_ref.at[f], b_at(u, shot), sb_sem.at[8 + i], b_sem.at[u, shot], {"shot": other, "surf": f})

    def a_wait(v, origin):
        pltpu.make_async_copy(a_at(v, origin), a_at(v, origin), a_sem.at[v, origin]).wait()

    def b_wait(v, origin):
        pltpu.make_async_copy(b_at(v, origin), b_at(v, origin), b_sem.at[v, origin]).wait()

    def a_right(v, origin):
        send(a_at(v, origin), a_at(v, origin), yr_sem.at[v, origin], a_sem.at[v, origin], right)

    def a_left(v, origin):
        send(a_at(v, origin), a_at(v, origin), yl_sem.at[v, origin], a_sem.at[v, origin], left)

    def b_right(v, origin):
        send(b_at(v, origin), b_at(v, origin), xr_sem.at[v, origin], b_sem.at[v, origin], xright)

    def b_left(v, origin):
        send(b_at(v, origin), b_at(v, origin), xl_sem.at[v, origin], b_sem.at[v, origin], xleft)

    def dot(v, h, ca, cb):
        here = pl.ds(pl.multiple_of(h * half, half), half)
        return lax.dot_general(
            a_buf[v, ca, here, :], b_buf[v, cb, here, :], (((0,), (0,)), ((), ())), preferred_element_type=jnp.float32
        )

    acc[...] = jnp.zeros_like(acc)

    def multiply(v, h):
        acc[0] += dot(v, h, 0, 0) - dot(v, h, 1, 1)
        acc[1] += dot(v, h, 0, 1) + dot(v, h, 1, 0)

    def b_pass(v, h, flip):
        if flip:
            b_wait(v, s_of(h, (x + 1) % 4))
            b_left(v, s_of(h, (x + 1) % 4))
        else:
            b_wait(v, s_of(h, (x + 3) % 4))
            b_right(v, s_of(h, (x + 3) % 4))

    def b_finish(v, h, flip):
        b_wait(v, s_of(h, (x + 3) % 4) if flip else s_of(h, (x + 1) % 4))
        b_wait(v, s_of(h, (x + 2) % 4))

    for t in range(12):
        if t < 8:
            v = surf_of(NEAR[t])
            a_wait(v, y)
            a_right(v, y)
            a_left(v, y)
            b_wait(v, shot)
            b_right(v, shot)
            b_left(v, shot)
            w = surf_of(FAR[t])
            b_wait(w, other)
            b_right(w, other)
            b_left(w, other)
        for lag in (1, 2, 3):
            q = t - lag
            if not 0 <= q < 8:
                continue
            v = surf_of(NEAR[q])
            before, after = (y + 8 - lag) % 8, (y + lag) % 8
            a_wait(v, before)
            if lag < 3 or q % 2 == 0:
                a_right(v, before)
            a_wait(v, after)
            if lag < 3 or q % 2 == 1:
                a_left(v, after)
            if lag == 1:
                b_pass(v, zh, q % 2 == 1)
                b_pass(surf_of(FAR[q]), 1 - zh, q % 2 == 0)
        q = t - 4
        if q >= 0:
            v = surf_of(NEAR[q])
            a_wait(v, (y + 4) % 8)
            b_finish(v, zh, q % 2 == 1)
            multiply(v, zh)
            b_finish(surf_of(FAR[q]), 1 - zh, q % 2 == 0)
            for m in range(8):
                if max(m, NEAR.index(FAR[m])) == q:
                    multiply(surf_of(FAR[m]), 1 - zh)
    out_ref[...] = acc[...]
    for copy in started:
        copy.wait_send()


def products(shot_data, recv_data):
    freqs, parts, rows, cols = shot_data.shape
    dma = pltpu.SemaphoreType.DMA
    return pl.pallas_call(
        kernel,
        out_shape=jax.ShapeDtypeStruct((parts, cols, cols), jnp.float32),
        in_specs=[pl.BlockSpec(memory_space=pl.ANY)] * 2,
        out_specs=pl.BlockSpec(memory_space=pltpu.VMEM),
        scratch_shapes=[
            pltpu.VMEM((freqs, parts, 8 * rows, cols), shot_data.dtype),
            pltpu.VMEM((freqs, parts, 8 * rows, cols), shot_data.dtype),
            pltpu.VMEM((parts, cols, cols), jnp.float32),
            dma((8, 8)),
            dma((8, 8)),
            dma((8,)),
            dma((16,)),
            dma((8, 8)),
            dma((8, 8)),
            dma((8, 8)),
            dma((8, 8)),
        ],
        compiler_params=pltpu.CompilerParams(
            collective_id=0, has_side_effects=True, vmem_limit_bytes=40 * 1024 * 1024
        ),
    )(shot_data, recv_data)


def on_device(shot_data, recv_data, shot_offset, recv_offset, shot_taper_index, receiver_taper_index):
    multiples = products(shot_data, recv_data)
    shot_row_block = shot_offset.shape[0]
    recv_cols = recv_offset.shape[0]
    shot_pos = (
        lax.axis_index("shot") * shot_row_block
        + jnp.arange(shot_row_block, dtype=jnp.int32)
        + shot_offset
    )
    recv_pos = (
        lax.axis_index("recv") * recv_cols + jnp.arange(recv_cols, dtype=jnp.int32) + recv_offset
    )
    distance = jnp.abs(recv_pos[None, :] - shot_pos[:, None])
    half_width = R // 8 * (2 + shot_taper_index[:, None] + receiver_taper_index[None, :])
    ratio = jnp.minimum(distance, half_width).astype(jnp.float32) / half_width.astype(jnp.float32)
    taper = 0.5 * (1.0 + jnp.cos(jnp.pi * ratio))
    return (multiples * taper[None, :, :])[None]


def solution(mesh):
    placed = (
        P(None, None, ("surf", "recv"), "shot"),
        P(None, None, ("surf", "shot"), "recv"),
        P("shot"),
        P("recv"),
        P("shot"),
        P("recv"),
    )
    return jax.shard_map(
        on_device,
        mesh=mesh,
        in_specs=placed,
        out_specs=P("surf", None, "shot", "recv"),
        check_vma=False,
    )
```

time: 371 us -> 106 us (0.29)
  the two profiles are of different devices: /device:TPU:2 before, /device:TPU:147 now
where the time goes in v1:
time: 106 us
  Pallas kernels  99.3 us (94%)
  local copies, waits for them, and re-layouts  4.31 us (4%)
  other arithmetic  1.94 us (2%)
    pallas_call x1, Pallas kernels, products(): pl.pallas_call(kernel, out_shape=jax.ShapeDtypeStruct((parts, cols, cols)...  99.3 us
    unnamed x12, local copies, waits for them, and re-layouts  4.31 us

profile of v1, /device:TPU:147, one launch (start us, length us, event | category | flops | bytes accessed | tf_op | source)
XLA Modules:
  0.0 105.6 jit_solution(11610553571084724022)
XLA Ops:
  0.0 0.0 copy-start.5
  0.0 0.7 copy-done.5
  0.7 0.0 copy-start.3
  0.7 0.0 copy-start.4
  0.7 0.7 copy-done.3
  1.4 0.0 copy-done.4
  1.4 0.0 copy-start.2
  1.4 0.7 copy-done.2
  2.1 1.1 %add_multiply_fusion = f32[256,256]{1,0:T(8,128)S(1)} fusion(s32[256]{0:T(256)S(1)} %copy-done.2, s32[256]{0:T(256)S(1)} %broadcast_add_fusion, s32[256]{0:T(256)S(1)} %get-tuple-element.5, s32[256]{0:T(256)S(1)} %get-tuple-element.6), kind=kLoop, calls=%fused_computation.1 | loop fusion | flops 720896 | bytes 266240 | tf_op jit(solution)/shard_map/mul | solution.py:204
  3.2 0.0 copy-start
  3.2 1.1 %copy-done = bf16[8,2,96,256]{3,2,1,0:T(8,128)(2,1)S(1)} copy-done((bf16[8,2,96,256]{3,2,1,0:T(8,128)(2,1)S(1)}, bf16[8,2,96,256]{3,2,1,0:T(8,128)(2,1)}, u32[]{:S(2)}) %copy-start) | copy-done | bytes 786456
  4.3 0.0 copy-start.1
  4.3 1.1 %copy-done.1 = bf16[8,2,96,256]{3,2,1,0:T(8,128)(2,1)S(1)} copy-done((bf16[8,2,96,256]{3,2,1,0:T(8,128)(2,1)S(1)}, bf16[8,2,96,256]{3,2,1,0:T(8,128)(2,1)}, u32[]{:S(2)}) %copy-start.1) | copy-done | bytes 786456
  5.4 99.3 %shard_map.64 = f32[2,256,256]{2,1,0:T(8,128)S(1)} custom-call(bf16[8,2,96,256]{3,2,1,0:T(8,128)(2,1)S(1)} %copy-done, bf16[8,2,96,256]{3,2,1,0:T(8,128)(2,1)S(1)} %copy-done.1), custom_call_target="tpu_custom_call" | custom-call | tf_op jit(solution)/shard_map/pallas_call | solution.py:165
  104.8 0.8 multiply_bitcast_fusion
  (2 shorter events, 0.0 us)
Async XLA Ops:
  0.0 0.7 copy-start.5
  0.7 0.7 copy-start.3
  0.7 0.7 copy-start.4
  1.4 0.7 copy-start.2
  3.2 1.1 %copy-start = (bf16[8,2,96,256]{3,2,1,0:T(8,128)(2,1)S(1)}, bf16[8,2,96,256]{3,2,1,0:T(8,128)(2,1)}, u32[]{:S(2)}) copy-start(bf16[8,2,96,256]{3,2,1,0:T(8,128)(2,1)} %s_ref.1) | copy-start | bytes 2359300
  4.3 1.1 %copy-start.1 = (bf16[8,2,96,256]{3,2,1,0:T(8,128)(2,1)S(1)}, bf16[8,2,96,256]{3,2,1,0:T(8,128)(2,1)}, u32[]{:S(2)}) copy-start(bf16[8,2,96,256]{3,2,1,0:T(8,128)(2,1)} %r_ref.1) | copy-start | bytes 2359300

commit v2 on v1

v2 whole, which is shorter than its diff:
```python
import jax
import jax.numpy as jnp
from jax import lax
from jax.experimental import pallas as pl
from jax.experimental.pallas import tpu as pltpu
from jax.sharding import PartitionSpec as P

NEAR = ((0, 0), (0, 1), (1, 0), (1, 1), (2, 0), (2, 1), (3, 0), (3, 1))
FAR = ((2, 0), (2, 1), (3, 0), (3, 1), (1, 0), (1, 1), (0, 0), (0, 1))
PROGRAM = (
    ('S', 0), ('S', 1), ('N', 1), ('F', 0), ('S', 2), ('S', 3), ('F', 1), ('S', 4),
    ('S', 5), ('N', 2), ('N', 3), ('S', 6), ('S', 7), ('F', 2), ('F', 3), ('N', 4),
    ('N', 5), ('F', 4), ('F', 5), ('N', 6), ('N', 7), ('F', 6), ('F', 7), ('t', 0),
    ('s', 0), ('n', 0), ('s', 1), ('y', 0, 1), ('n', 1), ('f', 0), ('xn', 0), ('s', 2),
    ('y', 1, 1), ('y', 0, 2), ('f', 1), ('xn', 1), ('xf', 0), ('en', 0), ('s', 3), ('y', 2, 1),
    ('y', 1, 2), ('y', 0, 3), ('n', 2), ('n', 3), ('xf', 1), ('en', 1), ('ef', 0), ('s', 4),
    ('y', 3, 1), ('y', 2, 2), ('y', 1, 3), ('f', 2), ('f', 3), ('xn', 2), ('xn', 3), ('e', 0),
    ('ef', 1), ('mn', 0), ('s', 5), ('y', 4, 1), ('y', 3, 2), ('y', 2, 3), ('n', 4), ('n', 5),
    ('xf', 2), ('xf', 3), ('e', 1), ('en', 2), ('en', 3), ('mn', 1), ('s', 6), ('y', 5, 1),
    ('y', 4, 2), ('y', 3, 3), ('f', 4), ('f', 5), ('xn', 4), ('xn', 5), ('e', 2), ('ef', 2),
    ('ef', 3), ('mn', 2), ('s', 7), ('y', 6, 1), ('y', 5, 2), ('y', 4, 3), ('n', 6), ('n', 7),
    ('xf', 4), ('xf', 5), ('e', 3), ('en', 4), ('en', 5), ('mn', 3), ('y', 7, 1), ('y', 6, 2),
    ('y', 5, 3), ('f', 6), ('f', 7), ('xn', 6), ('xn', 7), ('e', 4), ('ef', 4), ('ef', 5),
    ('mn', 4), ('mf', 0), ('mf', 4), ('mf', 5), ('y', 7, 2), ('y', 6, 3), ('xf', 6), ('xf', 7),
    ('e', 5), ('en', 6), ('en', 7), ('mn', 5), ('mf', 1), ('y', 7, 3), ('e', 6), ('ef', 6),
    ('ef', 7), ('mn', 6), ('mf', 2), ('mf', 6), ('mf', 7), ('e', 7), ('mn', 7), ('mf', 3),
)
MESH = pl.DeviceIdType.MESH


def kernel(
    s_ref, r_ref, so_ref, ro_ref, si_ref, ri_ref, out_ref,
    a_buf, b_buf, acc, taper, ints, a_sem, b_sem, z_sem, yr_sem, yl_sem, xr_sem, xl_sem, i_sem,
):
    shot = lax.axis_index("shot")
    y = lax.axis_index("recv")
    u = lax.axis_index("surf")
    zh, x = shot // 4, shot % 4
    zl, c = u // 2, u % 2
    rows = s_ref.shape[2]
    cols = s_ref.shape[3]
    half = 4 * rows

    def turn(b):
        if b == 1:
            return zl + 1 - 2 * (zl % 2)
        return 3 - zl if b == 3 else (zl + b) % 4

    def surf_of(step):
        b, e = step
        return turn(b) * 2 + (c + e) % 2

    dest_of = surf_of

    def a_at(v, origin):
        return a_buf.at[v, :, pl.ds(pl.multiple_of(origin * rows, rows), rows), :]

    def b_at(v, origin):
        return b_buf.at[v, :, pl.ds(pl.multiple_of(origin * rows, rows), rows), :]

    def s_of(h, xx):
        return h * 4 + xx

    right = {"recv": (y + 1) % 8}
    left = {"recv": (y + 7) % 8}
    xright = {"shot": s_of(zh, (x + 1) % 4)}
    xleft = {"shot": s_of(zh, (x + 3) % 4)}
    other = s_of(1 - zh, x)

    tables = (so_ref, ro_ref, si_ref, ri_ref)
    for i, table in enumerate(tables):
        pltpu.make_async_copy(table, ints.at[i], i_sem.at[i]).start()
    pltpu.make_async_copy(s_ref.at[u], a_at(u, y), a_sem.at[u, y]).start()
    pltpu.make_async_copy(r_ref.at[u], b_at(u, shot), b_sem.at[u, shot]).start()

    barrier = pltpu.get_barrier_semaphore()
    peers = [right, left, xright, xleft]
    for step in NEAR:
        f = dest_of(step)
        if step != (0, 0):
            peers.append({"surf": f})
        peers.append({"shot": other, "surf": f})
    for peer in peers:
        pl.semaphore_signal(barrier, inc=1, device_id=peer, device_id_type=MESH)
    pl.semaphore_wait(barrier, len(peers))

    started = []

    def send(src, dst, send_sem, recv_sem, device):
        copy = pltpu.make_async_remote_copy(
            src_ref=src, dst_ref=dst, send_sem=send_sem, recv_sem=recv_sem, device_id=device, device_id_type=MESH
        )
        copy.start()
        started.append(copy)

    def a_wait(v, origin):
        pltpu.make_async_copy(a_at(v, origin), a_at(v, origin), a_sem.at[v, origin]).wait()

    def b_wait(v, origin):
        pltpu.make_async_copy(b_at(v, origin), b_at(v, origin), b_sem.at[v, origin]).wait()

    def a_right(v, origin):
        send(a_at(v, origin), a_at(v, origin), yr_sem.at[v, origin], a_sem.at[v, origin], right)

    def a_left(v, origin):
        send(a_at(v, origin), a_at(v, origin), yl_sem.at[v, origin], a_sem.at[v, origin], left)

    def b_right(v, origin):
        send(b_at(v, origin), b_at(v, origin), xr_sem.at[v, origin], b_sem.at[v, origin], xright)

    def b_left(v, origin):
        send(b_at(v, origin), b_at(v, origin), xl_sem.at[v, origin], b_sem.at[v, origin], xleft)

    def dot(v, h, ca, cb):
        here = pl.ds(pl.multiple_of(h * half, half), half)
        return lax.dot_general(
            a_buf[v, ca, here, :], b_buf[v, cb, here, :], (((0,), (0,)), ((), ())), preferred_element_type=jnp.float32
        )

    def multiply(v, h):
        acc[0] += dot(v, h, 0, 0) - dot(v, h, 1, 1)
        acc[1] += dot(v, h, 0, 1) + dot(v, h, 1, 0)

    def prepare():
        acc[...] = jnp.zeros_like(acc)
        for i, table in enumerate(tables):
            pltpu.make_async_copy(table, ints.at[i], i_sem.at[i]).wait()

        def rows_of(i):
            return jnp.broadcast_to(ints[pl.ds(i, 1), :].astype(jnp.float32), (cols, cols))

        lane = lax.broadcasted_iota(jnp.int32, (cols, cols), 1)
        shot_pos = (rows_of(0) + (lane + shot * cols).astype(jnp.float32)).T
        recv_pos = rows_of(1) + (lane + y * cols).astype(jnp.float32)
        distance = jnp.abs(recv_pos - shot_pos)
        width = 256.0 * (2.0 + rows_of(2).T + rows_of(3))
        taper[...] = 0.5 * (1.0 + jnp.cos(jnp.pi * (jnp.minimum(distance, width) / width)))

    def run(op):
        kind, i = op[0], op[1]
        if kind == "S" and i > 0:
            f = dest_of(NEAR[i])
            send(s_ref.at[f], a_at(u, y), z_sem.at[0, i], a_sem.at[u, y], {"surf": f})
        elif kind == "N" and i > 0:
            f = dest_of(NEAR[i])
            send(r_ref.at[f], b_at(u, shot), z_sem.at[1, i], b_sem.at[u, shot], {"surf": f})
        elif kind == "F":
            f = dest_of(FAR[i])
            send(r_ref.at[f], b_at(u, shot), z_sem.at[2, i], b_sem.at[u, shot], {"shot": other, "surf": f})
        elif kind == "s":
            v = surf_of(NEAR[i])
            a_wait(v, y)
            a_right(v, y)
            a_left(v, y)
        elif kind == "y":
            lag = op[2]
            v = surf_of(NEAR[i])
            before, after = (y + 8 - lag) % 8, (y + lag) % 8
            a_wait(v, before)
            if lag < 3 or i % 2 == 0:
                a_right(v, before)
            a_wait(v, after)
            if lag < 3 or i % 2 == 1:
                a_left(v, after)
        elif kind == "e":
            a_wait(surf_of(NEAR[i]), (y + 4) % 8)
        elif kind in ("n", "f"):
            v = surf_of((NEAR if kind == "n" else FAR)[i])
            origin = shot if kind == "n" else other
            b_wait(v, origin)
            b_right(v, origin)
            b_left(v, origin)
        elif kind in ("xn", "xf", "en", "ef"):
            near = kind[1] == "n"
            v = surf_of((NEAR if near else FAR)[i])
            h = zh if near else 1 - zh
            flip = (i % 2 == 1) == near
            if kind[0] == "x":
                if flip:
                    b_wait(v, s_of(h, (x + 1) % 4))
                    b_left(v, s_of(h, (x + 1) % 4))
                else:
                    b_wait(v, s_of(h, (x + 3) % 4))
                    b_right(v, s_of(h, (x + 3) % 4))
            else:
                b_wait(v, s_of(h, (x + 3) % 4) if flip else s_of(h, (x + 1) % 4))
                b_wait(v, s_of(h, (x + 2) % 4))
        elif kind == "mn":
            multiply(surf_of(NEAR[i]), zh)
        elif kind == "mf":
            multiply(surf_of(FAR[i]), 1 - zh)
        elif kind == "t":
            prepare()

    for op in PROGRAM:
        run(op)
    out_ref[...] = acc[...] * taper[...][None]
    for copy in started:
        copy.wait_send()


def predict(*args):
    freqs, parts, rows, cols = args[0].shape
    dma = pltpu.SemaphoreType.DMA
    return pl.pallas_call(
        kernel,
        out_shape=jax.ShapeDtypeStruct((parts, cols, cols), jnp.float32),
        in_specs=[pl.BlockSpec(memory_space=pl.ANY)] * 6,
        out_specs=pl.BlockSpec(memory_space=pltpu.VMEM),
        scratch_shapes=[
            pltpu.VMEM((freqs, parts, 8 * rows, cols), args[0].dtype),
            pltpu.VMEM((freqs, parts, 8 * rows, cols), args[0].dtype),
            pltpu.VMEM((parts, cols, cols), jnp.float32),
            pltpu.VMEM((cols, cols), jnp.float32),
            pltpu.VMEM((4, cols), jnp.int32),
            dma((8, 8)),
            dma((8, 8)),
            dma((3, 8)),
            dma((8, 8)),
            dma((8, 8)),
            dma((8, 8)),
            dma((8, 8)),
            dma((4,)),
        ],
        compiler_params=pltpu.CompilerParams(
            collective_id=0, has_side_effects=True, vmem_limit_bytes=60 * 1024 * 1024
        ),
    )(*args)


def solution(mesh):
    placed = (
        P(None, None, ("surf", "recv"), "shot"),
        P(None, None, ("surf", "shot"), "recv"),
        P("shot"),
        P("recv"),
        P("shot"),
        P("recv"),
    )
    return jax.shard_map(
        lambda *args: predict(*args)[None],
        mesh=mesh,
        in_specs=placed,
        out_specs=P("surf", None, "shot", "recv"),
        check_vma=False,
    )
```

time: 106 us -> 93.3 us (0.88)
  the two profiles are of different devices: /device:TPU:147 before, /device:TPU:80 now
where the time goes in v2:
time: 93.3 us; the launch traced here: 93.1 us
  Pallas kernels  91.2 us (98%)
  local copies, waits for them, and re-layouts  1.87 us (2%)
    pallas_call x1, Pallas kernels, predict(): pl.pallas_call(kernel, out_shape=jax.ShapeDtypeStruct((parts, cols, cols)...  91.2 us
    unnamed x1, local copies, waits for them, and re-layouts  1.87 us

profile of v2, /device:TPU:80, one launch (start us, length us, event | category | flops | bytes accessed | tf_op | source)
XLA Modules:
  0.0 93.1 jit_solution(966553396191327727)
XLA Ops:
  0.0 91.2 %shard_map.64 = f32[2,256,256]{2,1,0:T(8,128)} custom-call(bf16[8,2,96,256]{3,2,1,0:T(8,128)(2,1)} %s_ref.1, bf16[8,2,96,256]{3,2,1,0:T(8,128)(2,1)} %r_ref.1, s32[256]{0:T(256)} %so_ref.1, s32[256]{0:T(256)} %ro_ref.1, s32[256]{0:T(256)} %si_ref.1, s32[256]{0:T(256)} %ri_ref.1), custom_call_target="tpu_custom_call" | custom-call | tf_op jit(solution)/shard_map/pallas_call | solution.py:205
  91.3 1.9 %copy.8 = f32[1,2,256,256]{3,2,1,0:T(8,128)} copy(f32[1,2,256,256]{3,2,1,0:T(8,128)} %bitcast.1) | data formatting | bytes 1048576

commit v3 on v2

--- a/solution.py
+++ b/solution.py
@@ -8,22 +8,22 @@
 NEAR = ((0, 0), (0, 1), (1, 0), (1, 1), (2, 0), (2, 1), (3, 0), (3, 1))
 FAR = ((2, 0), (2, 1), (3, 0), (3, 1), (1, 0), (1, 1), (0, 0), (0, 1))
 PROGRAM = (
-    ('S', 0), ('S', 1), ('N', 1), ('F', 0), ('S', 2), ('S', 3), ('F', 1), ('S', 4),
-    ('S', 5), ('N', 2), ('N', 3), ('S', 6), ('S', 7), ('F', 2), ('F', 3), ('N', 4),
-    ('N', 5), ('F', 4), ('F', 5), ('N', 6), ('N', 7), ('F', 6), ('F', 7), ('t', 0),
-    ('s', 0), ('n', 0), ('s', 1), ('y', 0, 1), ('n', 1), ('f', 0), ('xn', 0), ('s', 2),
-    ('y', 1, 1), ('y', 0, 2), ('f', 1), ('xn', 1), ('xf', 0), ('en', 0), ('s', 3), ('y', 2, 1),
-    ('y', 1, 2), ('y', 0, 3), ('n', 2), ('n', 3), ('xf', 1), ('en', 1), ('ef', 0), ('s', 4),
-    ('y', 3, 1), ('y', 2, 2), ('y', 1, 3), ('f', 2), ('f', 3), ('xn', 2), ('xn', 3), ('e', 0),
-    ('ef', 1), ('mn', 0), ('s', 5), ('y', 4, 1), ('y', 3, 2), ('y', 2, 3), ('n', 4), ('n', 5),
-    ('xf', 2), ('xf', 3), ('e', 1), ('en', 2), ('en', 3), ('mn', 1), ('s', 6), ('y', 5, 1),
-    ('y', 4, 2), ('y', 3, 3), ('f', 4), ('f', 5), ('xn', 4), ('xn', 5), ('e', 2), ('ef', 2),
-    ('ef', 3), ('mn', 2), ('s', 7), ('y', 6, 1), ('y', 5, 2), ('y', 4, 3), ('n', 6), ('n', 7),
-    ('xf', 4), ('xf', 5), ('e', 3), ('en', 4), ('en', 5), ('mn', 3), ('y', 7, 1), ('y', 6, 2),
-    ('y', 5, 3), ('f', 6), ('f', 7), ('xn', 6), ('xn', 7), ('e', 4), ('ef', 4), ('ef', 5),
-    ('mn', 4), ('mf', 0), ('mf', 4), ('mf', 5), ('y', 7, 2), ('y', 6, 3), ('xf', 6), ('xf', 7),
-    ('e', 5), ('en', 6), ('en', 7), ('mn', 5), ('mf', 1), ('y', 7, 3), ('e', 6), ('ef', 6),
-    ('ef', 7), ('mn', 6), ('mf', 2), ('mf', 6), ('mf', 7), ('e', 7), ('mn', 7), ('mf', 3),
+    ('S', 1), ('N', 1), ('S', 2), ('S', 3), ('F', 0), ('F', 1), ('N', 2), ('N', 3),
+    ('S', 4), ('S', 5), ('F', 2), ('F', 3), ('S', 6), ('S', 7), ('N', 4), ('N', 5),
+    ('F', 4), ('F', 5), ('N', 6), ('N', 7), ('F', 6), ('F', 7), ('s', 0), ('n', 0),
+    ('s', 1), ('y', 0, 1), ('n', 1), ('xn', 0), ('s', 2), ('y', 1, 1), ('y', 0, 2), ('f', 0),
+    ('f', 1), ('xn', 1), ('en', 0), ('s', 3), ('y', 2, 1), ('y', 1, 2), ('y', 0, 3), ('n', 2),
+    ('n', 3), ('xf', 0), ('xf', 1), ('en', 1), ('s', 4), ('y', 3, 1), ('y', 2, 2), ('y', 1, 3),
+    ('f', 2), ('f', 3), ('xn', 2), ('xn', 3), ('e', 0), ('ef', 0), ('ef', 1), ('mn', 0),
+    ('s', 5), ('y', 4, 1), ('y', 3, 2), ('y', 2, 3), ('n', 4), ('n', 5), ('xf', 2), ('xf', 3),
+    ('e', 1), ('en', 2), ('en', 3), ('mn', 1), ('s', 6), ('y', 5, 1), ('y', 4, 2), ('y', 3, 3),
+    ('f', 4), ('f', 5), ('xn', 4), ('xn', 5), ('e', 2), ('ef', 2), ('ef', 3), ('mn', 2),
+    ('s', 7), ('y', 6, 1), ('y', 5, 2), ('y', 4, 3), ('n', 6), ('n', 7), ('xf', 4), ('xf', 5),
+    ('e', 3), ('en', 4), ('en', 5), ('mn', 3), ('y', 7, 1), ('y', 6, 2), ('y', 5, 3), ('f', 6),
+    ('f', 7), ('xn', 6), ('xn', 7), ('e', 4), ('ef', 4), ('ef', 5), ('mn', 4), ('mf', 0),
+    ('mf', 4), ('mf', 5), ('y', 7, 2), ('y', 6, 3), ('xf', 6), ('xf', 7), ('e', 5), ('en', 6),
+    ('en', 7), ('mn', 5), ('mf', 1), ('y', 7, 3), ('e', 6), ('ef', 6), ('ef', 7), ('mn', 6),
+    ('mf', 2), ('mf', 6), ('mf', 7), ('e', 7), ('mn', 7), ('mf', 3),
 )
 MESH = pl.DeviceIdType.MESH
 
@@ -74,15 +74,11 @@
     pltpu.make_async_copy(r_ref.at[u], b_at(u, shot), b_sem.at[u, shot]).start()
 
     barrier = pltpu.get_barrier_semaphore()
-    peers = [right, left, xright, xleft]
-    for step in NEAR:
-        f = dest_of(step)
-        if step != (0, 0):
-            peers.append({"surf": f})
-        peers.append({"shot": other, "surf": f})
+    peers = [{"shot": other, "surf": dest_of(step)} for step in NEAR]
+    peers += [{"surf": dest_of(step)} for step in NEAR[:0:-1]]
+    peers += [right, left, xright, xleft]
     for peer in peers:
         pl.semaphore_signal(barrier, inc=1, device_id=peer, device_id_type=MESH)
-    pl.semaphore_wait(barrier, len(peers))
 
     started = []
 
@@ -189,9 +185,9 @@
             multiply(surf_of(NEAR[i]), zh)
         elif kind == "mf":
             multiply(surf_of(FAR[i]), 1 - zh)
-        elif kind == "t":
-            prepare()
-
+
+    prepare()
+    pl.semaphore_wait(barrier, len(peers))
     for op in PROGRAM:
         run(op)
     out_ref[...] = acc[...] * taper[...][None]
@@ -223,9 +219,9 @@
             dma((4,)),
         ],
         compiler_params=pltpu.CompilerParams(
-            collective_id=0, has_side_effects=True, vmem_limit_bytes=60 * 1024 * 1024
+            collective_id=0, has_side_effects=True, vmem_limit_bytes=40 * 1024 * 1024
         ),
-    )(*args)
+    )(*(pltpu.with_memory_space_constraint(a, pltpu.HBM) for a in args))
 
 
 def solution(mesh):

time: 93.3 us -> 91.1 us (0.976)
  the two profiles are of different devices: /device:TPU:80 before, /device:TPU:144 now
where the time goes in v3:
time: 91.1 us; the launch traced here: 90.9 us
  Pallas kernels  90.1 us (99%)
    pallas_call x1, Pallas kernels, predict(): pl.pallas_call(kernel, out_shape=jax.ShapeDtypeStruct((parts, cols, cols)...  90.1 us

profile of v3, /device:TPU:144, one launch (start us, length us, event | category | flops | bytes accessed | tf_op | source)
XLA Modules:
  0.0 90.9 jit_solution(8933597072051961543)
XLA Ops:
  0.0 90.1 %shard_map.64 = f32[2,256,256]{2,1,0:T(8,128)S(1)} custom-call(bf16[8,2,96,256]{3,2,1,0:T(8,128)(2,1)} %s_ref.1, bf16[8,2,96,256]{3,2,1,0:T(8,128)(2,1)} %r_ref.1, s32[256]{0:T(256)} %so_ref.1, s32[256]{0:T(256)} %ro_ref.1, s32[256]{0:T(256)} %si_ref.1, s32[256]{0:T(256)} %ri_ref.1), custom_call_target="tpu_custom_call" | custom-call | tf_op jit(solution)/shard_map/pallas_call | solution.py:201
  90.1 0.8 copy.8

commit v4 on v3

--- a/solution.py
+++ b/solution.py
@@ -1,3 +1,5 @@
+import functools
+
 import jax
 import jax.numpy as jnp
 from jax import lax
@@ -9,7 +11,7 @@
 FAR = ((2, 0), (2, 1), (3, 0), (3, 1), (1, 0), (1, 1), (0, 0), (0, 1))
 PROGRAM = (
     ('S', 1), ('N', 1), ('S', 2), ('S', 3), ('F', 0), ('F', 1), ('N', 2), ('N', 3),
-    ('S', 4), ('S', 5), ('F', 2), ('F', 3), ('S', 6), ('S', 7), ('N', 4), ('N', 5),
+    ('S', 4), ('S', 5), ('F', 2), ('F', 3), ('N', 4), ('N', 5), ('S', 6), ('S', 7),
     ('F', 4), ('F', 5), ('N', 6), ('N', 7), ('F', 6), ('F', 7), ('s', 0), ('n', 0),
     ('s', 1), ('y', 0, 1), ('n', 1), ('xn', 0), ('s', 2), ('y', 1, 1), ('y', 0, 2), ('f', 0),
     ('f', 1), ('xn', 1), ('en', 0), ('s', 3), ('y', 2, 1), ('y', 1, 2), ('y', 0, 3), ('n', 2),
@@ -107,15 +109,13 @@
     def b_left(v, origin):
         send(b_at(v, origin), b_at(v, origin), xl_sem.at[v, origin], b_sem.at[v, origin], xleft)
 
-    def dot(v, h, ca, cb):
+    def multiply(v, h):
         here = pl.ds(pl.multiple_of(h * half, half), half)
-        return lax.dot_general(
-            a_buf[v, ca, here, :], b_buf[v, cb, here, :], (((0,), (0,)), ((), ())), preferred_element_type=jnp.float32
-        )
-
-    def multiply(v, h):
-        acc[0] += dot(v, h, 0, 0) - dot(v, h, 1, 1)
-        acc[1] += dot(v, h, 0, 1) + dot(v, h, 1, 0)
+        left_re, left_im = a_buf[v, 0, here, :].T, a_buf[v, 1, here, :].T
+        right_re, right_im = b_buf[v, 0, here, :], b_buf[v, 1, here, :]
+        dot = functools.partial(jnp.dot, preferred_element_type=jnp.float32)
+        acc[0] += dot(left_re, right_re) - dot(left_im, right_im)
+        acc[1] += dot(left_re, right_im) + dot(left_im, right_re)
 
     def prepare():
         acc[...] = jnp.zeros_like(acc)

time: 91.1 us -> 90.5 us (level)
  the two profiles are of different devices: /device:TPU:144 before, /device:TPU:24 now
where the time goes in v4:
time: 90.5 us; the launch traced here: 90.3 us
  Pallas kernels  89.5 us (99%)
    pallas_call x1, Pallas kernels, predict(): pl.pallas_call(kernel, out_shape=jax.ShapeDtypeStruct((parts, cols, cols)...  89.5 us

profile of v4, /device:TPU:24, one launch (start us, length us, event | category | flops | bytes accessed | tf_op | source)
XLA Modules:
  0.0 90.3 jit_solution(4233812243654210386)
XLA Ops:
  0.0 89.5 %shard_map.64 = f32[2,256,256]{2,1,0:T(8,128)S(1)} custom-call(bf16[8,2,96,256]{3,2,1,0:T(8,128)(2,1)} %s_ref.1, bf16[8,2,96,256]{3,2,1,0:T(8,128)(2,1)} %r_ref.1, s32[256]{0:T(256)} %so_ref.1, s32[256]{0:T(256)} %ro_ref.1, s32[256]{0:T(256)} %si_ref.1, s32[256]{0:T(256)} %ri_ref.1), custom_call_target="tpu_custom_call" | custom-call | tf_op jit(solution)/shard_map/pallas_call | solution.py:201
  89.5 0.8 copy.8

commit v5 on v4

--- a/solution.py
+++ b/solution.py
@@ -24,8 +24,8 @@
     ('e', 3), ('en', 4), ('en', 5), ('mn', 3), ('y', 7, 1), ('y', 6, 2), ('y', 5, 3), ('f', 6),
     ('f', 7), ('xn', 6), ('xn', 7), ('e', 4), ('ef', 4), ('ef', 5), ('mn', 4), ('mf', 0),
     ('mf', 4), ('mf', 5), ('y', 7, 2), ('y', 6, 3), ('xf', 6), ('xf', 7), ('e', 5), ('en', 6),
-    ('en', 7), ('mn', 5), ('mf', 1), ('y', 7, 3), ('e', 6), ('ef', 6), ('ef', 7), ('mn', 6),
-    ('mf', 2), ('mf', 6), ('mf', 7), ('e', 7), ('mn', 7), ('mf', 3),
+    ('en', 7), ('mn', 5), ('mf', 1), ('y', 7, 3), ('e', 6), ('ef', 6), ('ef', 7),
+    ('mw', 6), ('mf', 6), ('mf', 7), ('e', 7),  ('mw', 7),
 )
 MESH = pl.DeviceIdType.MESH
 
@@ -110,7 +110,7 @@
         send(b_at(v, origin), b_at(v, origin), xl_sem.at[v, origin], b_sem.at[v, origin], xleft)
 
     def multiply(v, h):
-        here = pl.ds(pl.multiple_of(h * half, half), half)
+        here = slice(None) if h is None else pl.ds(pl.multiple_of(h * half, half), half)
         left_re, left_im = a_buf[v, 0, here, :].T, a_buf[v, 1, here, :].T
         right_re, right_im = b_buf[v, 0, here, :], b_buf[v, 1, here, :]
         dot = functools.partial(jnp.dot, preferred_element_type=jnp.float32)
@@ -183,6 +183,8 @@
                 b_wait(v, s_of(h, (x + 2) % 4))
         elif kind == "mn":
             multiply(surf_of(NEAR[i]), zh)
+        elif kind == "mw":
+            multiply(surf_of(NEAR[i]), None)
         elif kind == "mf":
             multiply(surf_of(FAR[i]), 1 - zh)
 

time: 90.5 us -> 90.3 us (level)
  no operation moved by 1% of the time
where the time goes in v5:
time: 90.3 us; the launch traced here: 90.2 us
  Pallas kernels  89.4 us (99%)
    pallas_call x1, Pallas kernels, predict(): pl.pallas_call(kernel, out_shape=jax.ShapeDtypeStruct((parts, cols, cols)...  89.4 us

profile of v5, /device:TPU:24, one launch (start us, length us, event | category | flops | bytes accessed | tf_op | source)
XLA Modules:
  0.0 90.2 jit_solution(9476022719082469970)
XLA Ops:
  0.0 89.4 %shard_map.64 = f32[2,256,256]{2,1,0:T(8,128)S(1)} custom-call(bf16[8,2,96,256]{3,2,1,0:T(8,128)(2,1)} %s_ref.1, bf16[8,2,96,256]{3,2,1,0:T(8,128)(2,1)} %r_ref.1, s32[256]{0:T(256)} %so_ref.1, s32[256]{0:T(256)} %ro_ref.1, s32[256]{0:T(256)} %si_ref.1, s32[256]{0:T(256)} %ri_ref.1), custom_call_target="tpu_custom_call" | custom-call | tf_op jit(solution)/shard_map/pallas_call | solution.py:203
  89.4 0.8 copy.8
